TPU v7x, 32 devices: a whole 2x2x4 slice. The times are simulated.
32 devices in a mesh: blk: 8 (over z, y), lblk: 4 (over x, core).
Axes of the slice: x: 2, y: 2, z: 4, core: 2. Of those that a mesh axis runs over, the one named last changes fastest.
Arguments:
- sky: bfloat16 [8, 2, 32, 16384], P(None, None, 'blk', 'lblk'), may hold values from -6 to 6
- arc_start: int32 [2, 32], P(None, 'blk'), may hold values from 0 to 16383
- arc_count: int32 [2, 32], P(None, 'blk'), may hold values from 4096 to 16384
- owner_modes: int32 [32], replicated, may hold values from 0 to 31, each once
- legendre: bfloat16 [32, 8, 4, 4096], P('blk', None, None, 'lblk'), may hold values from -1 to 1
Outputs:
- alm: float32 [8, 2, 32, 4096], P(None, None, 'blk', 'lblk')
Inputs may be any that keep to these rules, and one draw needn't show every extreme that they name: `owner_modes`: each m-mode 0 to 31 appears exactly once.
All inputs are finite; a program needn't handle non-finite values.
Results may differ from a plain program's by a relative error of at most 0.0049.
Values may be sent and summed in bfloat16 or wider, within the bound.
No kernel may reach another device: no remote copies, remote signals or barrier semaphores. Data moves between devices by JAX's collectives and lax.ppermute only.
A program may use at most 64 MiB of HBM per device.

v0:
```python
import math
import jax
import jax.numpy as jnp
from jax import lax
from jax.sharding import PartitionSpec as P

RLEN = 16384
DIFFUSION = 0.2


def padded(x, sides, width, wrap):
    for axis, dim in sides:
        count, length = (lax.axis_size(axis), x.shape[dim])
        up = [(i, (i + 1) % count) for i in range(count if wrap else count - 1)]
        down = [(j, i) for i, j in up]
        last = lax.slice_in_dim(x, length - width, length, axis=dim)
        initial = lax.slice_in_dim(x, 0, width, axis=dim)
        before = lax.ppermute(last, axis, up)
        after = lax.ppermute(initial, axis, down)
        x = jnp.concatenate([before, x, after], axis=dim)
    return x


def mode_basis(positions, mode_list):
    product_index = jnp.mod(positions[:, None] * mode_list[None, :], RLEN)
    angles = 2.0 * math.pi / RLEN * product_index.astype(jnp.float32)
    return (jnp.cos(angles).astype(jnp.bfloat16), (-jnp.sin(angles)).astype(jnp.bfloat16))


def legendre_section(fourier, legendre_rows, my_modes, degrees):
    north_part = fourier[:, 0].astype(jnp.float32)
    south_part = fourier[:, 1].astype(jnp.float32)
    folded = jnp.concatenate([north_part + south_part, north_part - south_part], axis=2).astype(
        jnp.bfloat16
    )
    latitude_sums = jnp.einsum(
        "xrys,srl->xysl", folded, legendre_rows, preferred_element_type=jnp.float32
    )
    even_parity = jnp.mod(degrees[None, :] + my_modes[:, None], 2) == 0
    chosen = jnp.where(even_parity[None, None], latitude_sums[:, :2], latitude_sums[:, 2:])
    inside = (degrees[None, :] >= my_modes[:, None])[None, None]
    return jnp.where(inside, chosen, jnp.zeros((), jnp.float32))


def local(sky, arc_start, arc_count, owner_modes, legendre):
    maps_here = sky.shape[0]
    band_here = sky.shape[2]
    quarter = sky.shape[3]
    column = lax.axis_index("lblk")
    positions = column * quarter + jnp.arange(quarter, dtype=jnp.int32)
    offset = jnp.mod(positions[None, None, :] - arc_start[:, :, None], RLEN)
    kept_mask = offset < arc_count[:, :, None]
    masked = jnp.where(kept_mask[None], sky, jnp.zeros((), jnp.bfloat16))
    layered = padded(masked, (("blk", 2),), 1, False)
    edge_padded = padded(masked, (("lblk", 3),), 1, True)
    is_last = lax.axis_index("blk") == lax.axis_size("blk") - 1
    beyond = jnp.where(is_last, masked[:, ::-1, band_here - 1 :], layered[:, :, band_here + 1 :])
    centre = masked.astype(jnp.float32)
    layer_above = layered[:, :, :band_here].astype(jnp.float32)
    layer_below = jnp.concatenate([layered[:, :, 2 : band_here + 1], beyond], axis=2).astype(
        jnp.float32
    )
    pixel_before = edge_padded[:, :, :, :quarter].astype(jnp.float32)
    pixel_after = edge_padded[:, :, :, 2:].astype(jnp.float32)
    total = layer_above + layer_below + pixel_before + pixel_after - 4.0 * centre
    smooth = (centre + DIFFUSION * total).astype(jnp.bfloat16)
    cos_table, sin_table = mode_basis(positions, owner_modes)
    slab_size = owner_modes.shape[0]
    flat_rows = smooth.reshape(maps_here * 2 * band_here, quarter)
    real_part = jnp.dot(flat_rows, cos_table, preferred_element_type=jnp.float32).reshape(
        maps_here, 2, band_here, slab_size
    )
    imag_part = jnp.dot(flat_rows, sin_table, preferred_element_type=jnp.float32).reshape(
        maps_here, 2, band_here, slab_size
    )
    parity = jnp.arange(band_here, dtype=jnp.int32) % 2
    phase_turn = math.pi / RLEN * (parity[:, None] * owner_modes[None, :]).astype(jnp.float32)
    turn_cos = jnp.cos(phase_turn)
    turn_sin = jnp.sin(phase_turn)
    norm_scale = 1.0 / math.sqrt(RLEN)
    rotated_real = (real_part * turn_cos + imag_part * turn_sin) * norm_scale
    rotated_imag = (imag_part * turn_cos - real_part * turn_sin) * norm_scale
    partial_value = jnp.stack([rotated_real, rotated_imag], axis=3)
    owned_count = legendre.shape[0]
    degree_part = legendre.shape[3]
    my_modes = lax.dynamic_slice_in_dim(
        owner_modes, lax.axis_index("blk") * owned_count, owned_count
    )
    degrees = column * degree_part + jnp.arange(degree_part, dtype=jnp.int32)
    legendre_rows = legendre.reshape(owned_count, -1, degree_part)
    spread = lax.all_to_all(partial_value, "blk", split_axis=4, concat_axis=2, tiled=True)
    summed = lax.psum(spread, "lblk")
    fourier = summed.astype(jnp.bfloat16)
    result = legendre_section(fourier, legendre_rows, my_modes, degrees)
    return result


def solution(mesh):
    return jax.shard_map(
        local,
        mesh=mesh,
        in_specs=(
            P(None, None, "blk", "lblk"),
            P(None, "blk"),
            P(None, "blk"),
            P(),
            P("blk", None, None, "lblk"),
        ),
        out_specs=P(None, None, "blk", "lblk"),
        check_vma=False,
    )
```

profile of v0, /device:TPU:0, one launch (start us, length us, event | category | flops | bytes accessed | tf_op | source)
XLA Modules:
  0.0 53.8 jit_solution(13409327666316147105)
XLA Ops:
  0.0 0.7 %copy-done.1 = s32[2,4]{1,0:T(2,128)S(1)} copy-done((s32[2,4]{1,0:T(2,128)S(1)}, s32[2,4]{1,0:T(2,128)}, u32[]{:S(2)}) %copy-start.1) | copy-done | bytes 56
  0.7 0.2 fusion.16
  0.9 1.3 %broadcast_select_fusion.1 = bf16[8,2,4,4096]{3,2,1,0:T(4,128)(2,1)S(1)} fusion(bf16[8,2,4,4096]{3,2,1,0:T(4,128)(2,1)} %param.5, pred[2,4,4096]{2,1,0:T(4,128)(4,1)S(1)} %fusion.16), kind=kLoop, calls=%fused_computation.20 | loop fusion | flops 262144 | bytes 1081344 | tf_op jit(solution)/shard_map/jit(_where)/select_n | solution.py:53
  2.2 0.6 %fusion.38 = (bf16[8,2,1,4096]{3,2,1,0:T(2,128)(2,1)S(1)}, bf16[8,2,1,4096]{3,2,1,0:T(2,128)(2,1)S(1)}) fusion(bf16[8,2,4,4096]{3,2,1,0:T(4,128)(2,1)S(1)} %broadcast_select_fusion.1), kind=kLoop, calls=%fused_computation.70 | loop fusion | bytes 524288 | tf_op jit(solution)/shard_map/slice | solution.py:17
  2.8 1.3 %collective-permute-start.1 = (bf16[8,2,1,4096]{3,2,1,0:T(2,128)(2,1)S(1)}, bf16[8,2,1,4096]{3,2,1,0:T(2,128)(2,1)S(1)}, u32[]{:S(2)}, u32[]{:S(2)}) collective-permute-start(bf16[8,2,1,4096]{3,2,1,0:T(2,128)(2,1)S(1)} %get-tuple-element.5), channel_id=1, source_target_pairs={{4,0},{8,4},{12,8},{16,12},{20,16},{24,20},{28,24},{5,1},{9,5},{13... | collective-permute-start | bytes 393224 | tf_op jit(solution)/shard_map/ppermute | solution.py:19
  4.1 5.5 %collective-permute-start = (bf16[8,2,1,4096]{3,2,1,0:T(2,128)(2,1)S(1)}, bf16[8,2,1,4096]{3,2,1,0:T(2,128)(2,1)S(1)}, u32[]{:S(2)}, u32[]{:S(2)}) collective-permute-start(bf16[8,2,1,4096]{3,2,1,0:T(2,128)(2,1)S(1)} %get-tuple-element.6), channel_id=1, source_target_pairs={{0,4},{4,8},{8,12},{12,16},{16,20},{20,24},{24,28},{1,5},{5,9},{9,... | collective-permute-start | bytes 393224 | tf_op jit(solution)/shard_map/ppermute | solution.py:18
  9.8 1.7 %collective-permute-start.3 = (bf16[8,2,4,1]{3,2,1,0:T(4,128)(2,1)S(1)}, bf16[8,2,4,1]{3,2,1,0:T(4,128)(2,1)S(1)}, u32[]{:S(2)}, u32[]{:S(2)}) collective-permute-start(bf16[8,2,4,1]{3,2,1,0:T(4,128)(2,1)S(1)} %get-tuple-element.8), channel_id=1, source_target_pairs={{1,0},{2,1},{3,2},{0,3},{5,4},{6,5},{7,6},{4,7},{9,8},{10,9},{11,1... | collective-permute-start | bytes 392 | tf_op jit(solution)/shard_map/ppermute | solution.py:19
  11.6 0.3 slice.52
  12.0 2.0 %collective-permute-done.1 = bf16[8,2,1,4096]{3,2,1,0:T(2,128)(2,1)S(1)} collective-permute-done((bf16[8,2,1,4096]{3,2,1,0:T(2,128)(2,1)S(1)}, bf16[8,2,1,4096]{3,2,1,0:T(2,128)(2,1)S(1)}, u32[]{:S(2)}, u32[]{:S(2)}) %collective-permute-start.1) | collective-permute-done | bytes 131104 | tf_op jit(solution)/shard_map/ppermute | solution.py:19
  14.0 0.4 broadcast_select_fusion
  14.4 5.3 %collective-permute-done = bf16[8,2,1,4096]{3,2,1,0:T(2,128)(2,1)S(1)} collective-permute-done((bf16[8,2,1,4096]{3,2,1,0:T(2,128)(2,1)S(1)}, bf16[8,2,1,4096]{3,2,1,0:T(2,128)(2,1)S(1)}, u32[]{:S(2)}, u32[]{:S(2)}) %collective-permute-start) | collective-permute-done | bytes 131104 | tf_op jit(solution)/shard_map/ppermute | solution.py:18
  19.7 2.3 %fusion.2 = bf16[8,2,4,4096]{3,2,1,0:T(4,128)(2,1)S(1)} fusion(bf16[8,2,4,4096]{3,2,1,0:T(4,128)(2,1)S(1)} %broadcast_select_fusion.1, bf16[8,2,4,1]{3,2,1,0:T(4,128)(2,1)S(1)} %collective-permute-done.3, bf16[8,2,4,1]{3,2,1,0:T(4,128)(2,1)S(1)} %collective-permute-done.2, bf16[8,2,1,4096]{3,2,1,0:T(2,128)(2,1)S(1)} %collective-permute-done, ...), kind=kLoop, calls=%fused_computation.5 | loop fusion | flops 6553600 | bytes 1704192 | tf_op jit(solution)/shard_map/convert_element_type | solution.py:66
  22.0 2.2 %fusion.7 = f32[8,2,4,32]{3,2,1,0:T(4,128)S(1)} fusion(bf16[8,2,4,4096]{3,2,1,0:T(4,128)(2,1)S(1)} %fusion.2, s32[32]{0:T(128)S(1)} %copy-done.3, s32[4096]{0:T(1024)S(1)} %iota_add_fusion), kind=kOutput, calls=%fused_computation.22 | convolution fusion | flops 18743296 | bytes 548992 | tf_op jit(solution)/shard_map/dot_general | solution.py:70
  24.3 2.3 %multiply_bitcast_fusion.1 = (f32[8,2,4,1,32]{4,2,1,0,3:T(4,128)S(1)}, f32[8,2,4,1,32]{4,2,1,0,3:T(4,128)S(1)}) fusion(f32[8,2,4,32]{3,2,1,0:T(4,128)S(1)} %fusion.7, f32[4,32]{1,0:T(4,128)S(1)} %get-tuple-element.16, f32[4,32]{1,0:T(4,128)S(1)} %get-tuple-element.15, bf16[8,2,4,4096]{3,2,1,0:T(4,128)(2,1)S(1)} %fusion.2, s32[32]{0:T(128)S(1)} %copy-done.3, ...), kind=kOutput, calls=%fused_computation.44 | convolution fusion | flops 18890752 | bytes 566400 | tf_op jit(solution)/shard_map/dot_general | solution.py:73
  26.6 0.2 copy.16
  26.8 0.9 %reshape.175 = f32[8,1,512]{2,1,0:T(1,128)} reshape(f32[32,2,2,4,8]{4,3,2,1,0:T(4,128)S(1)} %bitcast.33) | data formatting | bytes 32768
  27.7 5.8 %all-to-all-start = ((f32[8,1,512]{2,1,0:T(1,128)}), f32[8,1,512]{2,1,0:T(1,128)S(1)}, u32[]{:S(2)}, u32[]{:S(2)}) async-start(f32[8,1,512]{2,1,0:T(1,128)} %reshape.175), calls=%async_computation | async-start | bytes 32768 | tf_op jit(solution)/shard_map/all_to_all | solution.py:91
  33.6 6.4 %all-to-all-done = f32[8,1,512]{2,1,0:T(1,128)S(1)} async-done(((f32[8,1,512]{2,1,0:T(1,128)}), f32[8,1,512]{2,1,0:T(1,128)S(1)}, u32[]{:S(2)}, u32[]{:S(2)}) %all-to-all-start) | async-done | bytes 16416 | tf_op jit(solution)/shard_map/all_to_all | solution.py:91
  40.0 0.5 broadcast.207
  40.5 0.7 %reduce = f32[8,512]{1,0:T(8,128)S(1)} reduce(f32[8,1,512]{2,1,0:T(1,128)S(1)} %all-to-all-done, f32[]{:T(128)} %broadcast.207), dimensions={1}, to_apply=%all_to_all.13.reduce_sub_computation | reduce | bytes 32772 | tf_op jit(solution)/shard_map/all_to_all | solution.py:91
  41.2 0.3 reshape.176
  42.0 10.7 %psum.7 = bf16[8,2,32,2,4]{2,0,3,4,1:T(8,128)(2,1)S(1)} all-reduce(f32[8,2,32,2,4]{2,0,3,4,1:T(8,128)S(1)} %copy.19), channel_id=1, replica_groups=mesh['blk'=8,'lblk'=4] {'lblk'}, use_global_device_ids=true, to_apply=%region_0.1 | all-reduce | flops 4096 | bytes 24576 | tf_op jit(solution)/shard_map/psum | solution.py:92
  52.7 0.2 convolution_bitcast_fusion
  52.9 0.9 %copy.20 = f32[8,2,4,1024]{3,2,1,0:T(4,128)} copy(f32[8,2,4,1024]{3,0,1,2:T(8,128)S(1)} %fusion.12) | data formatting | bytes 524288 | tf_op jit(solution)/shard_map/jit(_where)/select_n | solution.py:42
  (24 shorter events, 1.0 us)
Async XLA Ops:
  0.0 0.7 %copy-start.1 = (s32[2,4]{1,0:T(2,128)S(1)}, s32[2,4]{1,0:T(2,128)}, u32[]{:S(2)}) copy-start(s32[2,4]{1,0:T(2,128)} %param.7) | copy-start | bytes 100
  0.0 0.7 %copy-start.2 = (s32[2,4]{1,0:T(2,128)S(1)}, s32[2,4]{1,0:T(2,128)}, u32[]{:S(2)}) copy-start(s32[2,4]{1,0:T(2,128)} %param.6) | copy-start | bytes 100
  2.8 11.2 %collective-permute-start.1 = (bf16[8,2,1,4096]{3,2,1,0:T(2,128)(2,1)S(1)}, bf16[8,2,1,4096]{3,2,1,0:T(2,128)(2,1)S(1)}, u32[]{:S(2)}, u32[]{:S(2)}) collective-permute-start(bf16[8,2,1,4096]{3,2,1,0:T(2,128)(2,1)S(1)} %get-tuple-element.5), channel_id=1, source_target_pairs={{4,0},{8,4},{12,8},{16,12},{20,16},{24,20},{28,24},{5,1},{9,5},{13... | collective-permute-start | bytes 393224 | tf_op jit(solution)/shard_map/ppermute | solution.py:19
  4.1 15.7 %collective-permute-start = (bf16[8,2,1,4096]{3,2,1,0:T(2,128)(2,1)S(1)}, bf16[8,2,1,4096]{3,2,1,0:T(2,128)(2,1)S(1)}, u32[]{:S(2)}, u32[]{:S(2)}) collective-permute-start(bf16[8,2,1,4096]{3,2,1,0:T(2,128)(2,1)S(1)} %get-tuple-element.6), channel_id=1, source_target_pairs={{0,4},{4,8},{8,12},{12,16},{16,20},{20,24},{24,28},{1,5},{5,9},{9,... | collective-permute-start | bytes 393224 | tf_op jit(solution)/shard_map/ppermute | solution.py:18
  9.7 4.7 %collective-permute-start.2 = (bf16[8,2,4,1]{3,2,1,0:T(4,128)(2,1)S(1)}, bf16[8,2,4,1]{3,2,1,0:T(4,128)(2,1)S(1)}, u32[]{:S(2)}, u32[]{:S(2)}) collective-permute-start(bf16[8,2,4,1]{3,2,1,0:T(4,128)(2,1)S(1)} %get-tuple-element.7), channel_id=1, source_target_pairs={{0,1},{1,2},{2,3},{3,0},{4,5},{5,6},{6,7},{7,4},{8,9},{9,10},{10,1... | collective-permute-start | bytes 392 | tf_op jit(solution)/shard_map/ppermute | solution.py:18
  9.8 1.7 %copy-start.3 = (s32[32]{0:T(128)S(1)}, s32[32]{0:T(128)}, u32[]{:S(2)}) copy-start(s32[32]{0:T(128)} %param.8) | copy-start | bytes 388
  9.8 4.6 %collective-permute-start.3 = (bf16[8,2,4,1]{3,2,1,0:T(4,128)(2,1)S(1)}, bf16[8,2,4,1]{3,2,1,0:T(4,128)(2,1)S(1)}, u32[]{:S(2)}, u32[]{:S(2)}) collective-permute-start(bf16[8,2,4,1]{3,2,1,0:T(4,128)(2,1)S(1)} %get-tuple-element.8), channel_id=1, source_target_pairs={{1,0},{2,1},{3,2},{0,3},{5,4},{6,5},{7,6},{4,7},{9,8},{10,9},{11,1... | collective-permute-start | bytes 392 | tf_op jit(solution)/shard_map/ppermute | solution.py:19
  26.6 7.0 %copy-start = (bf16[4,8,4,1024]{3,2,1,0:T(4,128)(2,1)S(1)}, bf16[4,8,4,1024]{3,2,1,0:T(4,128)(2,1)}, u32[]{:S(2)}) copy-start(bf16[4,8,4,1024]{3,2,1,0:T(4,128)(2,1)} %param.9) | copy-start | bytes 786436
  27.7 12.4 %all-to-all-start = ((f32[8,1,512]{2,1,0:T(1,128)}), f32[8,1,512]{2,1,0:T(1,128)S(1)}, u32[]{:S(2)}, u32[]{:S(2)}) async-start(f32[8,1,512]{2,1,0:T(1,128)} %reshape.175), calls=%async_computation | async-start | bytes 32768 | tf_op jit(solution)/shard_map/all_to_all | solution.py:91
where the time goes:
time: 54.1 us; the launch traced here: 53.8 us
  starting transfers between devices  14.4 us (27%)
  waiting for transfers between devices  13.7 us (25%)
  blocking collectives  10.7 us (20%)
  other arithmetic  5.17 us (10%)
  local copies, waits for them, and re-layouts  4.95 us (9%)
  matrix products  4.74 us (9%)
    psum x1, blocking collectives, local(): summed = lax.psum(spread, 'lblk')  10.7 us
    all_to_all x1, waiting for transfers between devices, local(): lax.all_to_all(partial_value, 'blk', split_axis=4, concat_axis=2, tiled=T...  6.4 us
    all_to_all x1, starting transfers between devices, local(): lax.all_to_all(partial_value, 'blk', split_axis=4, concat_axis=2, tiled=T...  5.78 us
    ppermute x2, starting transfers between devices, padded(): before = lax.ppermute(last, axis, up)  5.6 us
    ppermute x2, waiting for transfers between devices, padded(): before = lax.ppermute(last, axis, up)  5.33 us
    ppermute x2, starting transfers between devices, padded(): after = lax.ppermute(initial, axis, down)  3.01 us
    dot_general x1, matrix products, local(): jnp.dot(flat_rows, sin_table, preferred_element_type=jnp.float32)  2.29 us
    convert_element_type x1, other arithmetic, local(): smooth = (centre + DIFFUSION * total).astype(jnp.bfloat16)  2.27 us
  transfers between devices with their start and end apart: 5, of which 3 were waited for; matrix products, arithmetic and copies ran while one was open for 2% of the time, Pallas kernels for 0%

commit v1 on v0

--- a/solution.py
+++ b/solution.py
@@ -89,7 +89,8 @@
     degrees = column * degree_part + jnp.arange(degree_part, dtype=jnp.int32)
     legendre_rows = legendre.reshape(owned_count, -1, degree_part)
     spread = lax.all_to_all(partial_value, "blk", split_axis=4, concat_axis=2, tiled=True)
-    summed = lax.psum(spread, "lblk")
+    local_part = jax.lax.all_gather(spread, "lblk")
+    summed = jnp.sum(local_part, axis=0)
     fourier = summed.astype(jnp.bfloat16)
     result = legendre_section(fourier, legendre_rows, my_modes, degrees)
     return result

time: 54.1 us -> 49.2 us (0.909)
  blocking collectives: 10.7 us -> 5.78 us
    psum x1 -> x0, blocking collectives: 10.7 us -> none  [local(): summed = lax.psum(spread, 'lblk')]
    all_gather x0 -> x1, blocking collectives: none -> 5.78 us  [local(): local_part = jax.lax.all_gather(spread, 'lblk')]
where the time goes in v1:
time: 49.2 us; the launch traced here: 48.9 us
  starting transfers between devices  14.4 us (29%)
  waiting for transfers between devices  13.7 us (28%)
  blocking collectives  5.78 us (12%)
  other arithmetic  5.2 us (11%)
  local copies, waits for them, and re-layouts  4.95 us (10%)
  matrix products  4.74 us (10%)
    all_to_all x1, waiting for transfers between devices, local(): lax.all_to_all(partial_value, 'blk', split_axis=4, concat_axis=2, tiled=T...  6.4 us
    all_to_all x1, starting transfers between devices, local(): lax.all_to_all(partial_value, 'blk', split_axis=4, concat_axis=2, tiled=T...  5.78 us
    all_gather x1, blocking collectives, local(): local_part = jax.lax.all_gather(spread, 'lblk')  5.78 us
    ppermute x2, starting transfers between devices, padded(): before = lax.ppermute(last, axis, up)  5.6 us
    ppermute x2, waiting for transfers between devices, padded(): before = lax.ppermute(last, axis, up)  5.33 us
    ppermute x2, starting transfers between devices, padded(): after = lax.ppermute(initial, axis, down)  3.01 us
    dot_general x1, matrix products, local(): jnp.dot(flat_rows, sin_table, preferred_element_type=jnp.float32)  2.29 us
    convert_element_type x1, other arithmetic, local(): smooth = (centre + DIFFUSION * total).astype(jnp.bfloat16)  2.27 us
  transfers between devices with their start and end apart: 5, of which 3 were waited for; matrix products, arithmetic and copies ran while one was open for 2% of the time, Pallas kernels for 0%

profile of v1, /device:TPU:0, one launch (start us, length us, event | category | flops | bytes accessed | tf_op | source)
XLA Modules:
  0.0 48.9 jit_solution(3487729245378203156)
XLA Ops:
  0.0 0.7 %copy-done.1 = s32[2,4]{1,0:T(2,128)S(1)} copy-done((s32[2,4]{1,0:T(2,128)S(1)}, s32[2,4]{1,0:T(2,128)}, u32[]{:S(2)}) %copy-start.1) | copy-done | bytes 56
  0.7 0.2 fusion.16
  0.9 1.3 %broadcast_select_fusion.1 = bf16[8,2,4,4096]{3,2,1,0:T(4,128)(2,1)S(1)} fusion(bf16[8,2,4,4096]{3,2,1,0:T(4,128)(2,1)} %param.5, pred[2,4,4096]{2,1,0:T(4,128)(4,1)S(1)} %fusion.16), kind=kLoop, calls=%fused_computation.20 | loop fusion | flops 262144 | bytes 1081344 | tf_op jit(solution)/shard_map/jit(_where)/select_n | solution.py:53
  2.2 0.6 %fusion.38 = (bf16[8,2,1,4096]{3,2,1,0:T(2,128)(2,1)S(1)}, bf16[8,2,1,4096]{3,2,1,0:T(2,128)(2,1)S(1)}) fusion(bf16[8,2,4,4096]{3,2,1,0:T(4,128)(2,1)S(1)} %broadcast_select_fusion.1), kind=kLoop, calls=%fused_computation.71 | loop fusion | bytes 524288 | tf_op jit(solution)/shard_map/slice | solution.py:17
  2.8 1.3 %collective-permute-start.1 = (bf16[8,2,1,4096]{3,2,1,0:T(2,128)(2,1)S(1)}, bf16[8,2,1,4096]{3,2,1,0:T(2,128)(2,1)S(1)}, u32[]{:S(2)}, u32[]{:S(2)}) collective-permute-start(bf16[8,2,1,4096]{3,2,1,0:T(2,128)(2,1)S(1)} %get-tuple-element.5), channel_id=1, source_target_pairs={{4,0},{8,4},{12,8},{16,12},{20,16},{24,20},{28,24},{5,1},{9,5},{13... | collective-permute-start | bytes 393224 | tf_op jit(solution)/shard_map/ppermute | solution.py:19
  4.1 5.5 %collective-permute-start = (bf16[8,2,1,4096]{3,2,1,0:T(2,128)(2,1)S(1)}, bf16[8,2,1,4096]{3,2,1,0:T(2,128)(2,1)S(1)}, u32[]{:S(2)}, u32[]{:S(2)}) collective-permute-start(bf16[8,2,1,4096]{3,2,1,0:T(2,128)(2,1)S(1)} %get-tuple-element.6), channel_id=1, source_target_pairs={{0,4},{4,8},{8,12},{12,16},{16,20},{20,24},{24,28},{1,5},{5,9},{9,... | collective-permute-start | bytes 393224 | tf_op jit(solution)/shard_map/ppermute | solution.py:18
  9.8 1.7 %collective-permute-start.3 = (bf16[8,2,4,1]{3,2,1,0:T(4,128)(2,1)S(1)}, bf16[8,2,4,1]{3,2,1,0:T(4,128)(2,1)S(1)}, u32[]{:S(2)}, u32[]{:S(2)}) collective-permute-start(bf16[8,2,4,1]{3,2,1,0:T(4,128)(2,1)S(1)} %get-tuple-element.8), channel_id=1, source_target_pairs={{1,0},{2,1},{3,2},{0,3},{5,4},{6,5},{7,6},{4,7},{9,8},{10,9},{11,1... | collective-permute-start | bytes 392 | tf_op jit(solution)/shard_map/ppermute | solution.py:19
  11.6 0.3 slice.52
  12.0 2.0 %collective-permute-done.1 = bf16[8,2,1,4096]{3,2,1,0:T(2,128)(2,1)S(1)} collective-permute-done((bf16[8,2,1,4096]{3,2,1,0:T(2,128)(2,1)S(1)}, bf16[8,2,1,4096]{3,2,1,0:T(2,128)(2,1)S(1)}, u32[]{:S(2)}, u32[]{:S(2)}) %collective-permute-start.1) | collective-permute-done | bytes 131104 | tf_op jit(solution)/shard_map/ppermute | solution.py:19
  14.0 0.4 broadcast_select_fusion
  14.4 5.3 %collective-permute-done = bf16[8,2,1,4096]{3,2,1,0:T(2,128)(2,1)S(1)} collective-permute-done((bf16[8,2,1,4096]{3,2,1,0:T(2,128)(2,1)S(1)}, bf16[8,2,1,4096]{3,2,1,0:T(2,128)(2,1)S(1)}, u32[]{:S(2)}, u32[]{:S(2)}) %collective-permute-start) | collective-permute-done | bytes 131104 | tf_op jit(solution)/shard_map/ppermute | solution.py:18
  19.7 2.3 %fusion.2 = bf16[8,2,4,4096]{3,2,1,0:T(4,128)(2,1)S(1)} fusion(bf16[8,2,4,4096]{3,2,1,0:T(4,128)(2,1)S(1)} %broadcast_select_fusion.1, bf16[8,2,4,1]{3,2,1,0:T(4,128)(2,1)S(1)} %collective-permute-done.3, bf16[8,2,4,1]{3,2,1,0:T(4,128)(2,1)S(1)} %collective-permute-done.2, bf16[8,2,1,4096]{3,2,1,0:T(2,128)(2,1)S(1)} %collective-permute-done, ...), kind=kLoop, calls=%fused_computation.5 | loop fusion | flops 6553600 | bytes 1704192 | tf_op jit(solution)/shard_map/convert_element_type | solution.py:66
  22.0 2.2 %fusion.7 = f32[8,2,4,32]{3,2,1,0:T(4,128)S(1)} fusion(bf16[8,2,4,4096]{3,2,1,0:T(4,128)(2,1)S(1)} %fusion.2, s32[32]{0:T(128)S(1)} %copy-done.3, s32[4096]{0:T(1024)S(1)} %iota_add_fusion), kind=kOutput, calls=%fused_computation.22 | convolution fusion | flops 18743296 | bytes 548992 | tf_op jit(solution)/shard_map/dot_general | solution.py:70
  24.3 2.3 %multiply_bitcast_fusion.1 = (f32[8,2,4,1,32]{4,2,1,0,3:T(4,128)S(1)}, f32[8,2,4,1,32]{4,2,1,0,3:T(4,128)S(1)}) fusion(f32[8,2,4,32]{3,2,1,0:T(4,128)S(1)} %fusion.7, f32[4,32]{1,0:T(4,128)S(1)} %get-tuple-element.16, f32[4,32]{1,0:T(4,128)S(1)} %get-tuple-element.15, bf16[8,2,4,4096]{3,2,1,0:T(4,128)(2,1)S(1)} %fusion.2, s32[32]{0:T(128)S(1)} %copy-done.3, ...), kind=kOutput, calls=%fused_computation.45 | convolution fusion | flops 18890752 | bytes 566400 | tf_op jit(solution)/shard_map/dot_general | solution.py:73
  26.6 0.2 copy.14
  26.8 0.9 %reshape.176 = f32[8,1,512]{2,1,0:T(1,128)} reshape(f32[32,2,2,4,8]{4,3,2,1,0:T(4,128)S(1)} %bitcast.33) | data formatting | bytes 32768
  27.7 5.8 %all-to-all-start = ((f32[8,1,512]{2,1,0:T(1,128)}), f32[8,1,512]{2,1,0:T(1,128)S(1)}, u32[]{:S(2)}, u32[]{:S(2)}) async-start(f32[8,1,512]{2,1,0:T(1,128)} %reshape.176), calls=%async_computation | async-start | bytes 32768 | tf_op jit(solution)/shard_map/all_to_all | solution.py:91
  33.6 6.4 %all-to-all-done = f32[8,1,512]{2,1,0:T(1,128)S(1)} async-done(((f32[8,1,512]{2,1,0:T(1,128)}), f32[8,1,512]{2,1,0:T(1,128)S(1)}, u32[]{:S(2)}, u32[]{:S(2)}) %all-to-all-start) | async-done | bytes 16416 | tf_op jit(solution)/shard_map/all_to_all | solution.py:91
  40.0 0.5 %broadcast.207 = f32[]{:T(128)} broadcast(f32[]{:T(128)} %constant.147), dimensions={} | broadcast | bytes 8 | tf_op jit(solution)/shard_map/all_to_all | solution.py:91
  40.5 0.7 %reduce = f32[8,512]{1,0:T(8,128)S(1)} reduce(f32[8,1,512]{2,1,0:T(1,128)S(1)} %all-to-all-done, f32[]{:T(128)} %broadcast.207), dimensions={1}, to_apply=%all_to_all.11.reduce_sub_computation | reduce | bytes 32772 | tf_op jit(solution)/shard_map/all_to_all | solution.py:91
  41.2 0.3 reshape.177
  42.0 5.8 %all_gather.7 = f32[4,8,2,32,2,4]{3,1,5,4,2,0:T(8,128)S(1)} all-gather(f32[1,8,2,32,2,4]{3,1,5,4,2,0:T(8,128)S(1)} %copy.17), channel_id=1, replica_groups=mesh['blk'=8,'lblk'=4] {'lblk'}, dimensions={0}, use_global_device_ids=true | all-gather | bytes 81920 | tf_op jit(solution)/shard_map/all_gather | solution.py:92
  47.8 0.2 convolution_bitcast_fusion
  48.1 0.9 %copy.20 = f32[8,2,4,1024]{3,2,1,0:T(4,128)} copy(f32[8,2,4,1024]{3,0,1,2:T(8,128)S(1)} %fusion.12) | data formatting | bytes 524288 | tf_op jit(solution)/shard_map/jit(_where)/select_n | solution.py:42
  (25 shorter events, 1.0 us)
Async XLA Ops:
  0.0 0.7 %copy-start.1 = (s32[2,4]{1,0:T(2,128)S(1)}, s32[2,4]{1,0:T(2,128)}, u32[]{:S(2)}) copy-start(s32[2,4]{1,0:T(2,128)} %param.7) | copy-start | bytes 100
  0.0 0.7 %copy-start.2 = (s32[2,4]{1,0:T(2,128)S(1)}, s32[2,4]{1,0:T(2,128)}, u32[]{:S(2)}) copy-start(s32[2,4]{1,0:T(2,128)} %param.6) | copy-start | bytes 100
  2.8 11.2 %collective-permute-start.1 = (bf16[8,2,1,4096]{3,2,1,0:T(2,128)(2,1)S(1)}, bf16[8,2,1,4096]{3,2,1,0:T(2,128)(2,1)S(1)}, u32[]{:S(2)}, u32[]{:S(2)}) collective-permute-start(bf16[8,2,1,4096]{3,2,1,0:T(2,128)(2,1)S(1)} %get-tuple-element.5), channel_id=1, source_target_pairs={{4,0},{8,4},{12,8},{16,12},{20,16},{24,20},{28,24},{5,1},{9,5},{13... | collective-permute-start | bytes 393224 | tf_op jit(solution)/shard_map/ppermute | solution.py:19
  4.1 15.7 %collective-permute-start = (bf16[8,2,1,4096]{3,2,1,0:T(2,128)(2,1)S(1)}, bf16[8,2,1,4096]{3,2,1,0:T(2,128)(2,1)S(1)}, u32[]{:S(2)}, u32[]{:S(2)}) collective-permute-start(bf16[8,2,1,4096]{3,2,1,0:T(2,128)(2,1)S(1)} %get-tuple-element.6), channel_id=1, source_target_pairs={{0,4},{4,8},{8,12},{12,16},{16,20},{20,24},{24,28},{1,5},{5,9},{9,... | collective-permute-start | bytes 393224 | tf_op jit(solution)/shard_map/ppermute | solution.py:18
  9.7 4.7 %collective-permute-start.2 = (bf16[8,2,4,1]{3,2,1,0:T(4,128)(2,1)S(1)}, bf16[8,2,4,1]{3,2,1,0:T(4,128)(2,1)S(1)}, u32[]{:S(2)}, u32[]{:S(2)}) collective-permute-start(bf16[8,2,4,1]{3,2,1,0:T(4,128)(2,1)S(1)} %get-tuple-element.7), channel_id=1, source_target_pairs={{0,1},{1,2},{2,3},{3,0},{4,5},{5,6},{6,7},{7,4},{8,9},{9,10},{10,1... | collective-permute-start | bytes 392 | tf_op jit(solution)/shard_map/ppermute | solution.py:18
  9.8 1.7 %copy-start.3 = (s32[32]{0:T(128)S(1)}, s32[32]{0:T(128)}, u32[]{:S(2)}) copy-start(s32[32]{0:T(128)} %param.8) | copy-start | bytes 388
  9.8 4.6 %collective-permute-start.3 = (bf16[8,2,4,1]{3,2,1,0:T(4,128)(2,1)S(1)}, bf16[8,2,4,1]{3,2,1,0:T(4,128)(2,1)S(1)}, u32[]{:S(2)}, u32[]{:S(2)}) collective-permute-start(bf16[8,2,4,1]{3,2,1,0:T(4,128)(2,1)S(1)} %get-tuple-element.8), channel_id=1, source_target_pairs={{1,0},{2,1},{3,2},{0,3},{5,4},{6,5},{7,6},{4,7},{9,8},{10,9},{11,1... | collective-permute-start | bytes 392 | tf_op jit(solution)/shard_map/ppermute | solution.py:19
  26.6 7.0 %copy-start = (bf16[4,8,4,1024]{3,2,1,0:T(4,128)(2,1)S(1)}, bf16[4,8,4,1024]{3,2,1,0:T(4,128)(2,1)}, u32[]{:S(2)}) copy-start(bf16[4,8,4,1024]{3,2,1,0:T(4,128)(2,1)} %param.9) | copy-start | bytes 786436
  27.7 12.4 %all-to-all-start = ((f32[8,1,512]{2,1,0:T(1,128)}), f32[8,1,512]{2,1,0:T(1,128)S(1)}, u32[]{:S(2)}, u32[]{:S(2)}) async-start(f32[8,1,512]{2,1,0:T(1,128)} %reshape.176), calls=%async_computation | async-start | bytes 32768 | tf_op jit(solution)/shard_map/all_to_all | solution.py:91
